TPU v7x, 512 devices: a whole 4x8x8 slice. The times are simulated.
512 devices in a mesh: rows: 32 (over x, z), cols: 16 (over y, core).
Axes of the slice: x: 4, y: 8, z: 8, core: 2. Of those that a mesh axis runs over, the one named last changes fastest.
Arguments:
- points: float32 [3, 131072], P(None, 'rows'), as said below
- targets: float32 [16, 131072], P(None, 'rows'), may hold values from -6 to 6
- landmarks: int32 [256], replicated, may hold values from 0 to 131071
- neighbours: int32 [1024, 18], P('rows'), may hold values from 0 to 1023, as said below
- counts: int32 [1024], P('rows'), may hold values from 1 to 18
- core_inverse: float32 [256, 256], replicated, as said below
Outputs:
- solution: float32 [16, 131072], P(None, 'rows')
- residual: float32 [16, 131072], P(None, 'rows')
Inputs may be any that keep to these rules, and one draw needn't show every extreme that they name: `neighbours`: for block b the first counts[b] entries are distinct blocks in ascending order, b among them, each within 12 blocks of b; b lists c exactly when c lists b; the remaining slots hold b. `points`: points of blocks that do not list each other are farther apart than 1. `core_inverse`: Symmetric; each diagonal entry exceeds the sum of the magnitudes of the other entries of its row.
All inputs are finite; a program needn't handle non-finite values.
Results may differ from a plain program's by a relative error of at most 0.0003.
Values sent between devices are 32-bit elements; how exact they have to be, the bound alone decides.
A program may use at most 64 MiB of HBM per device.

v0:
```python
import jax
import jax.numpy as jnp
from jax import lax
from jax.sharding import PartitionSpec as P

MOST = 6
ITERS = 2


kernel_scale = 0.03125
ridge_shift = 1.0
tile_group = 32


def extended(cells, sides, width):
    for axis, dim in sides:
        count = lax.axis_size(axis)
        ends = count - 1
        head = lax.slice_in_dim(cells, 0, width, axis=dim)
        tail = lax.slice_in_dim(cells, cells.shape[dim] - width, cells.shape[dim], axis=dim)
        cells = jnp.concatenate(
            [
                lax.ppermute(tail, axis, [(i, (i + 1) % count) for i in range(ends)]),
                cells,
                lax.ppermute(head, axis, [((i + 1) % count, i) for i in range(ends)]),
            ],
            axis=dim,
        )
    return cells


def wendland(squared):
    distance = jnp.sqrt(squared)
    remain = jnp.maximum(1.0 - distance, 0.0)
    return remain * remain * remain * remain * (4.0 * distance + 1.0)


def squared_gap(first_pts, second_pts):
    offsets = first_pts[:, :, None] - second_pts[:, None, :]
    return jnp.sum(offsets * offsets, axis=0)


def tile_products(vector_halo, point_halo, row_points, nearby, amounts, last_tile):
    block_count = row_points.shape[1]
    block_width = row_points.shape[2]
    slot_count = nearby.shape[1]
    tile_ends = jnp.cumsum(amounts)
    tile_starts = tile_ends - amounts
    lane_ids = jnp.arange(tile_group, dtype=jnp.int32)
    block_ids = jnp.arange(block_count, dtype=jnp.int32)
    turn_count = (last_tile + tile_group - 1) // tile_group

    def advance(turn_index, running):
        position = turn_index * tile_group + lane_ids
        inside = position < last_tile
        owner_block = jnp.sum((tile_ends[None, :] <= position[:, None]).astype(jnp.int32), axis=1)
        owner_block = jnp.minimum(owner_block, block_count - 1)
        column = jnp.clip(position - tile_starts[owner_block], 0, slot_count - 1)
        partner = nearby[owner_block, column]
        row_side = row_points[:, owner_block]
        col_side = point_halo[:, partner]
        offsets = row_side[:, :, :, None] - col_side[:, :, None, :]
        kernel_tiles = wendland(jnp.sum(offsets * offsets, axis=0)) * inside[:, None, None].astype(
            jnp.float32
        )
        contrib = jnp.einsum(
            "ogn,gmn->ogm", vector_halo[:, partner], kernel_tiles, precision=lax.Precision.HIGHEST
        )
        placing = ((owner_block[:, None] == block_ids[None, :]) & inside[:, None]).astype(
            jnp.float32
        )
        return running + jnp.einsum(
            "ogm,gb->obm", contrib, placing, precision=lax.Precision.HIGHEST
        )

    start_total = jnp.zeros((vector_halo.shape[0], block_count, block_width), jnp.float32)
    return lax.fori_loop(0, turn_count, advance, start_total)


def body(points, targets, landmarks, neighbours, counts, core_inverse):
    col_count = lax.axis_size("cols")
    row_index = lax.axis_index("rows")
    col_index = lax.axis_index("cols")
    block_count = neighbours.shape[0]
    slab_points = points.shape[1]
    block_width = slab_points // block_count
    share_blocks = block_count // col_count
    share_points = share_blocks * block_width
    outputs_count = targets.shape[0]
    reach = 2 * MOST
    first_block = row_index * block_count
    local_ids = landmarks - row_index * slab_points
    present = (local_ids >= 0) & (local_ids < slab_points)
    picked = jnp.take(points, jnp.clip(local_ids, 0, slab_points - 1), axis=1) * present[
        None, :
    ].astype(jnp.float32)
    landmark_coords = lax.psum(picked, "rows")
    share_start = col_index * share_points
    own_points = lax.dynamic_slice_in_dim(points, share_start, share_points, 1)
    landmark_kernel = kernel_scale * wendland(squared_gap(landmark_coords, own_points))

    def precondition_share(residual_share):
        projected = jnp.dot(residual_share, landmark_kernel.T, precision=lax.Precision.HIGHEST)
        projected = lax.psum(projected, ("rows", "cols"))
        weights = jnp.dot(projected, core_inverse, precision=lax.Precision.HIGHEST)
        shared = residual_share - jnp.dot(weights, landmark_kernel, precision=lax.Precision.HIGHEST)
        product = lax.psum(jnp.sum(residual_share * shared, axis=1), ("rows", "cols"))
        return (shared, product)

    point_halo = extended(points, (("rows", 1),), reach * block_width)
    point_halo = point_halo.reshape(3, -1, block_width)
    nearby = neighbours - (first_block - reach)

    def share_of(vector):
        return lax.dynamic_slice_in_dim(vector, share_start, share_points, 1)

    def precondition(residual):
        shared, product = precondition_share(share_of(residual))
        return (lax.all_gather(shared, "cols", axis=1, tiled=True), product)

    solution = jnp.zeros_like(targets)
    residual = targets
    preconditioned, current = precondition(residual)
    direction = preconditioned
    for iteration in range(ITERS):
        vector_halo = extended(direction, (("rows", 1),), reach * block_width)
        vector_halo = vector_halo.reshape(outputs_count, -1, block_width)
        own_lists = lax.dynamic_slice_in_dim(nearby, col_index * share_blocks, share_blocks, 0)
        amounts = lax.dynamic_slice_in_dim(counts, col_index * share_blocks, share_blocks, 0)
        rows_here = own_points.reshape(3, share_blocks, block_width)
        tile_total = jnp.sum(amounts)
        partial_rows = tile_products(
            vector_halo, point_halo, rows_here, own_lists, amounts, tile_total
        )
        operate_product = lax.all_gather(
            partial_rows.reshape(outputs_count, share_points), "cols", axis=1, tiled=True
        )
        applied = kernel_scale * operate_product + ridge_shift * direction
        curvature_part = jnp.sum(share_of(direction) * share_of(applied), axis=1)
        step_size = current / lax.psum(curvature_part, ("rows", "cols"))
        solution = solution + step_size[:, None] * direction
        residual = residual - step_size[:, None] * applied
        if iteration + 1 < ITERS:
            preconditioned, following = precondition(residual)
            direction = preconditioned + (following / current)[:, None] * direction
            current = following
    solution, residual = (solution, residual)
    return (solution, residual)


def solution(mesh):
    placed = (P(None, "rows"), P(None, "rows"), P(), P("rows", None), P("rows"), P())
    return jax.shard_map(
        body,
        mesh=mesh,
        in_specs=placed,
        out_specs=(P(None, "rows"), P(None, "rows")),
        check_vma=False,
    )
```

profile of v0, /device:TPU:1, one launch (start us, length us, event | category | flops | bytes accessed | tf_op | source)
XLA Modules:
  0.0 766.5 jit_solution(12587315131149481955)
XLA Ops:
  0.7 0.8 fusion.98
  1.5 4.8 collective-permute-start
  6.3 1.3 collective-permute-start.1
  7.6 1.5 copy.37
  10.1 121.2 %psum.49 = f32[3,256]{0,1:T(8,128)S(1)} all-reduce(f32[3,256]{0,1:T(8,128)S(1)} %multiply_bitcast_fusion), channel_id=1, replica_groups=mesh['rows'=32,'cols'=16] {'rows'}, use_global_device_ids=true, to_apply=%region_0.1 | all-reduce | flops 768 | bytes 6144 | tf_op jit(solution)/shard_map/psum | solution.py:97
  132.0 124.0 %psum.50 = f32[16,256]{1,0:T(8,128)S(1)} all-reduce(f32[16,256]{1,0:T(8,128)S(1)} %fusion.84), channel_id=1, replica_groups=mesh['rows'=32,'cols'=16] {'rows','cols'}, use_global_device_ids=true, to_apply=%region_2.3 | all-reduce | flops 4096 | bytes 32768 | tf_op jit(solution)/shard_map/psum | solution.py:104
  256.7 16.2 %all_gather.12 = f32[16,4096]{1,0:T(8,128)S(1)} all-gather(f32[16,256]{1,0:T(8,128)S(1)} %get-tuple-element.306), channel_id=1, replica_groups=mesh['rows'=32,'cols'=16] {'cols'}, dimensions={1}, use_global_device_ids=true | all-gather | bytes 278528 | tf_op jit(solution)/shard_map/all_gather | solution.py:119
  272.9 2.8 collective-permute-start.2
  275.7 1.3 collective-permute-start.3
  277.3 0.8 bitcast_subtract_fusion
  279.0 2.5 collective-permute-done.3
  281.6 12.1 %while.22 = (s32[]{:T(128)}, f32[16,2,128]{2,1,0:T(2,128)S(1)}, s32[]{:T(128)}, s32[2]{0:T(128)S(1)}, s32[]{:T(128)}, /*index=5*/f32[3,2,128]{2,0,1:T(4,128)S(1)...) while((s32[]{:T(128)}, f32[16,2,128]{2,1,0:T(2,128)S(1)}, ...), condition=%wide.region_10.11_spmd.clone, body=%wide.region_7.10_spmd.clone.sunk | while | flops 111156288 | bytes 6040561 | solution.py:77
  282.3 1.3 fusion.136
  283.6 0.8 gather_fusion
  287.0 2.1 multiply_reduce_fusion.9
  289.0 4.3 fusion.139
  293.7 16.3 %all_gather.13 = f32[16,4096]{1,0:T(8,128)S(1)} all-gather(f32[16,256]{1,0:T(8,128)S(1)} %bitcast.164), channel_id=1, replica_groups=mesh['rows'=32,'cols'=16] {'cols'}, dimensions={1}, use_global_device_ids=true | all-gather | bytes 278528 | tf_op jit(solution)/shard_map/all_gather | solution.py:135
  310.1 105.2 %all-reduce = (f32[16]{0:T(128)S(1)}, f32[16]{0:T(128)S(1)}) all-reduce(f32[16]{0:T(128)S(1)} %get-tuple-element.305, f32[16]{0:T(128)S(1)} %multiply_reduce_fusion.5), channel_id=1, replica_groups=mesh['rows'=32,'cols'=16] {'rows','cols'}, use_global_device_ids=true, to_apply=%region_4.5 | all-reduce | flops 32 | bytes 256 | tf_op jit(solution)/shard_map/psum | solution.py:107
  415.8 94.5 %psum.53 = f32[16,256]{1,0:T(8,128)S(1)} all-reduce(f32[16,256]{1,0:T(8,128)S(1)} %fusion.82), channel_id=1, replica_groups=mesh['rows'=32,'cols'=16] {'rows','cols'}, use_global_device_ids=true, to_apply=%region_13.14 | all-reduce | flops 4096 | bytes 32768 | tf_op jit(solution)/shard_map/psum | solution.py:104
  511.0 95.3 %psum.54 = f32[16]{0:T(128)S(1)} all-reduce(f32[16]{0:T(128)S(1)} %get-tuple-element.307), channel_id=1, replica_groups=mesh['rows'=32,'cols'=16] {'rows','cols'}, use_global_device_ids=true, to_apply=%region_15.16 | all-reduce | flops 16 | bytes 128 | tf_op jit(solution)/shard_map/psum | solution.py:107
  606.4 18.3 %all_gather.14 = f32[16,4096]{1,0:T(8,128)S(1)} all-gather(f32[16,256]{1,0:T(8,128)S(1)} %get-tuple-element.308), channel_id=1, replica_groups=mesh['rows'=32,'cols'=16] {'cols'}, dimensions={1}, use_global_device_ids=true | all-gather | bytes 278528 | tf_op jit(solution)/shard_map/all_gather | solution.py:119
  624.7 1.3 collective-permute-start.4
  626.0 1.3 collective-permute-start.5
  627.3 0.9 collective-permute-done.4
  628.3 3.8 collective-permute-done.5
  632.2 12.0 %while.23 = (s32[]{:T(128)}, f32[16,2,128]{2,1,0:T(2,128)S(1)}, s32[]{:T(128)}, s32[2]{0:T(128)S(1)}, s32[]{:T(128)}, /*index=5*/f32[3,2,128]{2,0,1:T(4,128)S(1)...) while((s32[]{:T(128)}, f32[16,2,128]{2,1,0:T(2,128)S(1)}, ...), condition=%wide.region_19.20_spmd.clone, body=%wide.region_16.19_spmd.clone.sunk | while | flops 111156288 | bytes 6040561 | solution.py:77
  632.9 1.3 fusion.147
  637.5 2.1 multiply_reduce_fusion.10
  639.6 4.3 fusion.150
  644.2 16.8 %all_gather.15 = f32[16,4096]{1,0:T(8,128)S(1)} all-gather(f32[16,256]{1,0:T(8,128)S(1)} %bitcast.165), channel_id=1, replica_groups=mesh['rows'=32,'cols'=16] {'cols'}, dimensions={1}, use_global_device_ids=true | all-gather | bytes 278528 | tf_op jit(solution)/shard_map/all_gather | solution.py:135
  661.2 104.3 %psum.55 = f32[16]{0:T(128)S(1)} all-reduce(f32[16]{0:T(128)S(1)} %multiply_reduce_fusion.3), channel_id=1, replica_groups=mesh['rows'=32,'cols'=16] {'rows','cols'}, use_global_device_ids=true, to_apply=%region_21.22 | all-reduce | flops 16 | bytes 128 | tf_op jit(solution)/shard_map/psum | solution.py:140
  765.5 0.9 multiply_subtract_fusion
  (80 shorter events, 12.2 us)
Async XLA Ops:
  0.6 255.4 %copy-start = (f32[256,256]{1,0:T(8,128)S(1)}, f32[256,256]{1,0:T(8,128)}, u32[]{:S(2)}) copy-start(f32[256,256]{1,0:T(8,128)} %param.15) | copy-start | bytes 786436
  0.6 8.5 %copy-start.1 = (f32[3,4096]{1,0:T(4,128)S(1)}, f32[3,4096]{1,0:T(4,128)}, u32[]{:S(2)}) copy-start(f32[3,4096]{1,0:T(4,128)} %param.10) | copy-start | bytes 147460
  0.7 8.5 %copy-start.4 = (s32[256]{0:T(256)S(1)}, s32[256]{0:T(256)}, u32[]{:S(2)}) copy-start(s32[256]{0:T(256)} %param.12) | copy-start | bytes 3076
  0.7 130.9 %copy-start.2 = (f32[16,4096]{1,0:T(8,128)S(1)}, f32[16,4096]{1,0:T(8,128)}, u32[]{:S(2)}) copy-start(f32[16,4096]{1,0:T(8,128)} %param.11) | copy-start | bytes 786436
  1.5 277.5 %collective-permute-start = (f32[3,1536]{1,0:T(4,128)S(1)}, f32[3,1536]{1,0:T(4,128)S(1)}, u32[]{:S(2)}, u32[]{:S(2)}) collective-permute-start(f32[3,1536]{1,0:T(4,128)S(1)} %get-tuple-element.298), channel_id=1, source_target_pairs={{0,16},{16,32},{32,48},{48,64},{64,80},{80,96},{96,112},{112,128},... | collective-permute-start | bytes 55304 | tf_op jit(solution)/shard_map/ppermute | solution.py:23
  6.3 272.6 %collective-permute-start.1 = (f32[3,1536]{1,0:T(4,128)S(1)}, f32[3,1536]{1,0:T(4,128)S(1)}, u32[]{:S(2)}, u32[]{:S(2)}) collective-permute-start(f32[3,1536]{1,0:T(4,128)S(1)} %get-tuple-element.299), channel_id=1, source_target_pairs={{16,0},{32,16},{48,32},{64,48},{80,64},{96,80},{112,96},{128,112},... | collective-permute-start | bytes 55304 | tf_op jit(solution)/shard_map/ppermute | solution.py:25
  9.1 267.9 %copy-start.5 = (s32[32]{0:T(128)S(1)}, s32[32]{0:T(128)}, u32[]{:S(2)}) copy-start(s32[32]{0:T(128)} %param.14) | copy-start | bytes 388
  9.1 269.0 %copy-start.3 = (s32[32,18]{0,1:T(8,128)S(1)}, s32[32,18]{0,1:T(8,128)}, u32[]{:S(2)}) copy-start(s32[32,18]{0,1:T(8,128)} %param.13) | copy-start | bytes 6916
  272.9 6.1 collective-permute-start.2
  275.7 5.8 collective-permute-start.3
  624.7 3.5 collective-permute-start.4
  626.0 6.1 collective-permute-start.5
where the time goes:
time: 769 us; the launch traced here: 766 us
  blocking collectives  712 us (93%)
  starting transfers between devices  12.8 us (2%)
  matrix products  11.3 us (1%)
  other arithmetic  11.2 us (1%)
  local copies, waits for them, and re-layouts  9.75 us (1%)
    psum x2, blocking collectives, precondition_share(): projected = lax.psum(projected, ('rows', 'cols'))  219 us
    psum x2, blocking collectives, precondition_share(): lax.psum(jnp.sum(residual_share * shared, axis=1), ('rows', 'cols'))  201 us
    psum x1, blocking collectives, body(): landmark_coords = lax.psum(picked, 'rows')  121 us
    psum x1, blocking collectives, body(): step_size = current / lax.psum(curvature_part, ('rows', 'cols'))  104 us
    all_gather x2, blocking collectives, precondition(): return (lax.all_gather(shared, 'cols', axis=1, tiled=True), product)  34.5 us
    all_gather x2, blocking collectives, body(): lax.all_gather(partial_rows.reshape(outputs_count, share_points), 'cols',...  33.2 us
  transfers between devices with their start and end apart: 6, of which 3 were waited for; matrix products, arithmetic and copies ran while one was open for 1% of the time, Pallas kernels for 0%

commit v1 on v0

v1 whole, which is shorter than its diff:
```python
import jax
import jax.numpy as jnp
from jax import lax
from jax.sharding import PartitionSpec as P

MOST = 6
REACH = 2 * MOST

kernel_scale = 0.03125
ridge_shift = 1.0


def wendland(squared):
    distance = jnp.sqrt(squared)
    remain = jnp.maximum(1.0 - distance, 0.0)
    square = remain * remain
    return square * square * (4.0 * distance + 1.0)


def kernel_matrix(first_pts, second_pts):
    squared = 0.0
    for dim in range(3):
        offsets = first_pts[dim][:, None] - second_pts[dim][None, :]
        squared = squared + offsets * offsets
    return wendland(squared)


def product(first, second):
    return jnp.dot(first, second, precision=lax.Precision.HIGHEST)


def total(part):
    part = jnp.sum(lax.all_gather(part, "cols"), axis=0)
    return jnp.sum(lax.all_gather(part, "rows"), axis=0)


def extended(cells, width):
    count = lax.axis_size("rows")
    tail = cells[:, cells.shape[1] - width :]
    head = cells[:, :width]
    return jnp.concatenate(
        [
            lax.ppermute(tail, "rows", [(i, i + 1) for i in range(count - 1)]),
            cells,
            lax.ppermute(head, "rows", [(i + 1, i) for i in range(count - 1)]),
        ],
        axis=1,
    )


def body(points, targets, landmarks, neighbours, counts, core_inverse):
    col_count = lax.axis_size("cols")
    row_count = lax.axis_size("rows")
    row_index = lax.axis_index("rows")
    col_index = lax.axis_index("cols")
    slab = points.shape[1]
    block = slab // neighbours.shape[0]
    share = slab // col_count
    outs = targets.shape[0]
    halo = REACH * block
    window = share + 2 * halo

    local_ids = landmarks - row_index * slab
    present = (local_ids >= 0) & (local_ids < slab)
    picked = jnp.take(points, jnp.clip(local_ids, 0, slab - 1), axis=1)
    picked = jnp.where(present[None, :], picked, 0.0)
    marks = jnp.sum(lax.all_gather(picked, "rows"), axis=0)

    wide = extended(jnp.concatenate([points, targets], axis=0), halo)
    place = jnp.arange(slab + 2 * halo, dtype=jnp.int32) - halo
    place = place + row_index * slab
    valid = ((place >= 0) & (place < slab * row_count)).astype(jnp.float32)[None, :]
    wide_points = wide[:3]
    wide_targets = wide[3:]

    def near(array):
        return lax.dynamic_slice_in_dim(array, col_index * share, window, 1)

    def own(array):
        return lax.dynamic_slice_in_dim(array, halo + col_index * share, share, 1)

    marks_wide = kernel_scale * kernel_matrix(marks, wide_points)
    band = kernel_scale * kernel_matrix(near(wide_points), own(wide_points))
    marks_own = own(marks_wide).T

    def operate(vector):
        return product(near(vector), band) + ridge_shift * own(vector)

    def dots(first, second):
        return jnp.sum(first * second, axis=1, keepdims=True)

    first_own = own(wide_targets)
    sums = total(
        jnp.concatenate(
            [product(first_own, marks_own), dots(first_own, first_own)], axis=1
        )
    )
    u0 = sums[:, :-1]
    w0 = product(u0, core_inverse)
    rz0 = sums[:, -1:] - dots(w0, u0)
    z0 = (wide_targets - product(w0, marks_wide)) * valid
    q0 = operate(z0)
    q0_wide = extended(lax.all_gather(q0, "cols", axis=1, tiled=True), halo)
    z0_own = own(z0)
    sums = total(jnp.concatenate([product(q0, marks_own), dots(z0_own, q0)], axis=1))
    curve0 = sums[:, -1:]
    alpha0 = rz0 / curve0
    u1 = u0 - alpha0 * sums[:, :-1]
    r1 = wide_targets - alpha0 * q0_wide
    z1 = (r1 - product(product(u1, core_inverse), marks_wide)) * valid
    w1 = operate(z1)
    z1_own = own(z1)
    r1_own = own(r1)
    sums = total(
        jnp.concatenate(
            [dots(r1_own, z1_own), dots(z1_own, w1), dots(z1_own, q0) + dots(z0_own, w1)],
            axis=1,
        )
    )
    w1_slab = lax.all_gather(w1, "cols", axis=1, tiled=True)
    rz1 = sums[:, :1]
    beta = rz1 / rz0
    curve1 = sums[:, 1:2] + beta * (sums[:, 2:] + beta * curve0)
    alpha1 = rz1 / curve1

    def inner(array):
        return array[:, halo : halo + slab]

    z0_slab = inner(z0)
    solution = alpha0 * z0_slab + alpha1 * (inner(z1) + beta * z0_slab)
    residual = inner(r1) - alpha1 * (w1_slab + beta * inner(q0_wide))
    return (solution, residual)


def solution(mesh):
    placed = (P(None, "rows"), P(None, "rows"), P(), P("rows", None), P("rows"), P())
    return jax.shard_map(
        body,
        mesh=mesh,
        in_specs=placed,
        out_specs=(P(None, "rows"), P(None, "rows")),
        check_vma=False,
    )
```

time: 769 us -> 355 us (0.46)
  blocking collectives: 712 us -> 281 us
  matrix products: 11.3 us -> 38.9 us
    psum x6 -> x0, blocking collectives: 645 us -> none  [the longest x2 219 us: precondition_share(): projected = lax.psum(projected, ('rows', 'cols'))]
    all_gather x4 -> x9, blocking collectives: 67.6 us -> 281 us  [the longest x3 112 us: total(): return jnp.sum(lax.all_gather(part, 'rows'), axis=0)]
    dot_general x10 -> x8, matrix products: 11.3 us -> 38.9 us  [product(): return jnp.dot(first, second, precision=lax.Precision.HIGHEST)]
  transfers between devices with their start and end apart: 6 -> 4, of which waited for: 3 -> 0; matrix products, arithmetic and copies ran while one was open for 1% -> 1% of each run, Pallas kernels for 0% -> 0%
where the time goes in v1:
time: 355 us; the launch traced here: 348 us
  blocking collectives  281 us (79%)
  matrix products  38.9 us (11%)
  other arithmetic  12.2 us (3%)
  starting transfers between devices  9.29 us (3%)
  local copies, waits for them, and re-layouts  6.06 us (2%)
    all_gather x3, blocking collectives, total(): return jnp.sum(lax.all_gather(part, 'rows'), axis=0)  112 us
    all_gather x3, blocking collectives, total(): part = jnp.sum(lax.all_gather(part, 'cols'), axis=0)  72.9 us
    all_gather x1, blocking collectives, body(): marks = jnp.sum(lax.all_gather(picked, 'rows'), axis=0)  40.2 us
    dot_general x8, matrix products, product(): return jnp.dot(first, second, precision=lax.Precision.HIGHEST)  38.9 us
    all_gather x1, blocking collectives, body(): w1_slab = lax.all_gather(w1, 'cols', axis=1, tiled=True)  28.3 us
    all_gather x1, blocking collectives, body(): q0_wide = extended(lax.all_gather(q0, 'cols', axis=1, tiled=True), halo)  27.3 us
  transfers between devices with their start and end apart: 4, of which 0 were waited for; matrix products, arithmetic and copies ran while one was open for 1% of the time, Pallas kernels for 0%

profile of v1, /device:TPU:1, one launch (start us, length us, event | category | flops | bytes accessed | tf_op | source)
XLA Modules:
  0.0 348.3 jit_solution(10601097981732835222)
XLA Ops:
  0.6 1.0 pad_maximum_fusion.2
  1.7 4.8 %collective-permute-start = (f32[19,1536]{1,0:T(8,128)S(1)}, f32[19,1536]{1,0:T(8,128)S(1)}, u32[]{:S(2)}, u32[]{:S(2)}) collective-permute-start(f32[19,1536]{1,0:T(8,128)S(1)} %get-tuple-element.16), channel_id=1, source_target_pairs={{0,16},{16,32},{32,48},{48,64},{64,80},{80,96},{96,112},{112,128},... | collective-permute-start | bytes 350216 | tf_op jit(solution)/shard_map/ppermute | solution.py:43
  6.5 1.3 collective-permute-start.1
  7.8 1.5 copy.32
  9.3 0.7 compare_and_fusion
  10.0 0.7 gather_fusion
  10.9 40.2 %all_gather.46 = f32[32,3,256]{2,1,0:T(4,128)S(1)} all-gather(f32[1,3,256]{2,1,0:T(4,128)S(1)} %copy.33), channel_id=1, replica_groups=mesh['rows'=32,'cols'=16] {'rows'}, dimensions={0}, use_global_device_ids=true | all-gather | bytes 101376 | tf_op jit(solution)/shard_map/all_gather | solution.py:67
  51.3 0.9 pad_maximum_fusion.3
  52.2 0.2 dynamic-slice_reduce_fusion.2
  52.4 1.0 pad_maximum_fusion
  53.7 1.0 pad_maximum_fusion.6
  54.7 5.6 %multiply_multiply_fusion = f32[256,7168]{1,0:T(8,128)S(1)} fusion(f32[7168]{0:T(1024)S(1)} %bitcast.41, f32[256]{0:T(256)S(1)} %bitcast.54, f32[7168]{0:T(1024)S(1)} %bitcast.44, f32[256]{0:T(256)S(1)} %bitcast.51, f32[7168]{0:T(1024)S(1)} %bitcast.38, f32[256]{0:T(256)S(1)} %bitcast.48), kind=kLoop, calls=%fused_computation.5 | loop fusion | flops 29360128 | bytes 7429120 | tf_op jit(solution)/shard_map/mul | solution.py:82
  60.3 3.0 copy-done.1
  63.3 0.3 fusion.11
  63.6 29.6 %all-gather = f32[256,257]{1,0:T(8,128)S(1)} all-gather(f32[16,257]{1,0:T(8,128)S(1)} %pad_maximum_fusion.7), channel_id=2, replica_groups=mesh['rows'=32,'cols'=16] {'cols'}, dimensions={0}, use_global_device_ids=true | all-gather | bytes 279616 | tf_op jit(solution)/shard_map/all_gather | solution.py:33
  93.2 37.0 %all-gather.1 = f32[512,257]{1,0:T(8,128)S(1)} all-gather(f32[16,257]{1,0:T(8,128)S(1)} %reduce_sum.128), channel_id=3, replica_groups=mesh['rows'=32,'cols'=16] {'rows'}, dimensions={0}, use_global_device_ids=true | all-gather | bytes 542784 | tf_op jit(solution)/shard_map/all_gather | solution.py:34
  130.3 0.3 multiply_reduce_fusion.5
  130.6 9.0 %fusion.1 = f32[16,7168]{1,0:T(8,128)S(1)} fusion(f32[16,256]{1,0:T(8,128)S(1)} %get-tuple-element.35, f32[7168]{0:T(1024)S(1)} %bitcast.42, f32[256]{0:T(256)S(1)} %bitcast.55, f32[7168]{0:T(1024)S(1)} %bitcast.45, f32[256]{0:T(256)S(1)} %bitcast.52, f32[7168]{0:T(1024)S(1)} %bitcast.39, f32[256]{0:T(256)S(1)} %bitcast.49, f32[7168]{0:T(1024)S(1)} %fusion.19, ...), kind=kOutput, calls=%fused_computation.4 | convolution fusion | flops 381911040 | bytes 1051648 | tf_op jit(solution)/shard_map/dot_general | solution.py:29
  139.6 14.7 %multiply_reduce_fusion.4 = (f32[16]{0:T(128)S(1)}, f32[16,256]{1,0:T(8,128)S(1)}) fusion(f32[16,7168]{1,0:T(8,128)S(1)} %fusion.1, s32[]{:T(128)S(6)} %select_n.42, f32[256]{0:T(256)S(1)} %bitcast.61, f32[3328]{0:T(1024)S(1)} %get-tuple-element.7, f32[256]{0:T(256)S(1)} %bitcast.63, f32[3328]{0:T(1024)S(1)} %get-tuple-element.6, f32[256]{0:T(256)S(1)} %bitcast.59, ...), kind=kOutput, calls=%fused_computation.46 | convolution fusion | flops 177221616 | bytes 298056 | tf_op jit(solution)/shard_map/dot_general | solution.py:29
  154.2 1.2 fusion.9
  155.5 27.3 %all_gather.55 = f32[16,4096]{1,0:T(8,128)S(1)} all-gather(f32[16,256]{1,0:T(8,128)S(1)} %get-tuple-element.33), channel_id=1, replica_groups=mesh['rows'=32,'cols'=16] {'cols'}, dimensions={1}, use_global_device_ids=true | all-gather | bytes 278528 | tf_op jit(solution)/shard_map/all_gather | solution.py:103
  182.9 1.9 collective-permute-start.2
  184.8 1.3 collective-permute-start.3
  186.1 16.7 %all-gather.2 = f32[256,257]{1,0:T(8,128)S(1)} all-gather(f32[16,257]{1,0:T(8,128)S(1)} %pad_maximum_fusion.8), channel_id=4, replica_groups=mesh['rows'=32,'cols'=16] {'cols'}, dimensions={0}, use_global_device_ids=true | all-gather | bytes 279616 | tf_op jit(solution)/shard_map/all_gather | solution.py:33
  202.8 41.0 %all-gather.3 = f32[512,257]{1,0:T(8,128)S(1)} all-gather(f32[16,257]{1,0:T(8,128)S(1)} %reduce_sum.132), channel_id=5, replica_groups=mesh['rows'=32,'cols'=16] {'rows'}, dimensions={0}, use_global_device_ids=true | all-gather | bytes 542784 | tf_op jit(solution)/shard_map/all_gather | solution.py:34
  244.0 0.2 fusion.21
  244.4 9.0 %fusion = f32[16,7168]{1,0:T(8,128)S(1)} fusion(f32[16,7168]{1,0:T(8,128)S(1)} %fusion.6, f32[16,256]{1,0:T(8,128)S(1)} %fusion.21, f32[7168]{0:T(1024)S(1)} %bitcast.43, f32[256]{0:T(256)S(1)} %bitcast.56, f32[7168]{0:T(1024)S(1)} %bitcast.46, f32[256]{0:T(256)S(1)} %bitcast.53, f32[7168]{0:T(1024)S(1)} %bitcast.40, f32[256]{0:T(256)S(1)} %bitcast.50, ...), kind=kOutput, calls=%fused_computation.2 | convolution fusion | flops 381911040 | bytes 1051648 | tf_op jit(solution)/shard_map/dot_general | solution.py:29
  253.4 4.3 %multiply_reduce_fusion.3 = (f32[16]{0:T(128)S(1)}, f32[16]{0:T(128)S(1)}, f32[16]{0:T(128)S(1)}, f32[16]{0:T(128)S(1)}, f32[16,256]{1,0:T(8,128)S(1)}) fusion(f32[16,7168]{1,0:T(8,128)S(1)} %fusion.6, s32[]{:T(128)S(6)} %select_n.42, f32[16,7168]{1,0:T(8,128)S(1)} %fusion, f32[16,256]{1,0:T(8,128)S(1)} %get-tuple-element.33, f32[16,7168]{1,0:T(8,128)S(1)} %fusion.1, ...), kind=kOutput, calls=%fused_computation.45 | convolution fusion | flops 177246144 | bytes 347400 | tf_op jit(solution)/shard_map/dot_general | solution.py:29
  257.7 26.6 %all-gather.6 = f32[16,16,3]{1,2,0:T(4,128)S(1)} all-gather(f32[1,16,3]{1,2,0:T(4,128)S(1)} %maximum_bitcast_fusion), channel_id=6, replica_groups=mesh['rows'=32,'cols'=16] {'cols'}, dimensions={0}, use_global_device_ids=true | all-gather | bytes 3264 | tf_op jit(solution)/shard_map/all_gather | solution.py:33
  284.3 34.0 %all-gather.7 = f32[32,16,3]{1,2,0:T(4,128)S(1)} all-gather(f32[1,16,3]{1,2,0:T(4,128)S(1)} %bitcast.47), channel_id=7, replica_groups=mesh['rows'=32,'cols'=16] {'rows'}, dimensions={0}, use_global_device_ids=true | all-gather | bytes 6336 | tf_op jit(solution)/shard_map/all_gather | solution.py:34
  318.7 28.3 %all_gather.60 = f32[16,4096]{1,0:T(8,128)S(1)} all-gather(f32[16,256]{1,0:T(8,128)S(1)} %get-tuple-element.36), channel_id=1, replica_groups=mesh['rows'=32,'cols'=16] {'cols'}, dimensions={1}, use_global_device_ids=true | all-gather | bytes 278528 | tf_op jit(solution)/shard_map/all_gather | solution.py:120
  347.1 1.0 slice_subtract_fusion
  (37 shorter events, 1.8 us)
Async XLA Ops:
  0.6 129.6 %copy-start = (f32[256,256]{1,0:T(8,128)S(1)}, f32[256,256]{1,0:T(8,128)}, u32[]{:S(2)}) copy-start(f32[256,256]{1,0:T(8,128)} %param.9) | copy-start | bytes 786436
  1.7 49.6 %collective-permute-start = (f32[19,1536]{1,0:T(8,128)S(1)}, f32[19,1536]{1,0:T(8,128)S(1)}, u32[]{:S(2)}, u32[]{:S(2)}) collective-permute-start(f32[19,1536]{1,0:T(8,128)S(1)} %get-tuple-element.16), channel_id=1, source_target_pairs={{0,16},{16,32},{32,48},{48,64},{64,80},{80,96},{96,112},{112,128},... | collective-permute-start | bytes 350216 | tf_op jit(solution)/shard_map/ppermute | solution.py:43
  6.5 44.8 %collective-permute-start.1 = (f32[19,1536]{1,0:T(8,128)S(1)}, f32[19,1536]{1,0:T(8,128)S(1)}, u32[]{:S(2)}, u32[]{:S(2)}) collective-permute-start(f32[19,1536]{1,0:T(8,128)S(1)} %get-tuple-element.17), channel_id=1, source_target_pairs={{16,0},{32,16},{48,32},{64,48},{80,64},{96,80},{112,96},{128,112},... | collective-permute-start | bytes 350216 | tf_op jit(solution)/shard_map/ppermute | solution.py:45
  60.3 3.0 copy-start.1
  182.9 61.3 %collective-permute-start.2 = (f32[16,1536]{1,0:T(8,128)S(1)}, f32[16,1536]{1,0:T(8,128)S(1)}, u32[]{:S(2)}, u32[]{:S(2)}) collective-permute-start(f32[16,1536]{1,0:T(8,128)S(1)} %get-tuple-element.18), channel_id=1, source_target_pairs={{0,16},{16,32},{32,48},{48,64},{64,80},{80,96},{96,112},{112,128},... | collective-permute-start | bytes 294920 | tf_op jit(solution)/shard_map/ppermute | solution.py:43
  184.8 59.5 %collective-permute-start.3 = (f32[16,1536]{1,0:T(8,128)S(1)}, f32[16,1536]{1,0:T(8,128)S(1)}, u32[]{:S(2)}, u32[]{:S(2)}) collective-permute-start(f32[16,1536]{1,0:T(8,128)S(1)} %get-tuple-element.19), channel_id=1, source_target_pairs={{16,0},{32,16},{48,32},{64,48},{80,64},{96,80},{112,96},{128,112},... | collective-permute-start | bytes 294920 | tf_op jit(solution)/shard_map/ppermute | solution.py:45

commit v2 on v1

v2 whole, which is shorter than its diff:
```python
import functools

import jax
import jax.numpy as jnp
from jax import lax
from jax.experimental import pallas as pl
from jax.experimental.pallas import tpu as pltpu
from jax.sharding import PartitionSpec as P

MOST = 6
REACH = 2 * MOST

kernel_scale = 0.03125
ridge_shift = 1.0

F32 = jnp.float32
BF16 = jnp.bfloat16
MESH = pl.DeviceIdType.MESH
PTS = 8


def halves(value):
    high = value.astype(BF16)
    return high, (value - high.astype(F32)).astype(BF16)


def product(value, high, low):
    rows = value.shape[0]
    value_high, value_low = halves(value)
    both = jnp.concatenate([value_high, value_low], axis=0)
    first = jnp.dot(both, high, preferred_element_type=F32)
    second = jnp.dot(value_high, low, preferred_element_type=F32)
    return first[:rows] + (first[rows:] + second)


def kernel_rows(column, lanes):
    squared = None
    for dim in range(3):
        offsets = column[:, dim : dim + 1] - lanes[dim : dim + 1, :]
        term = offsets * offsets
        squared = term if squared is None else squared + term
    distance = squared * lax.rsqrt(jnp.maximum(squared, 1e-30))
    remain = jnp.maximum(1.0 - distance, 0.0)
    square = remain * remain
    return (square * square) * ((4.0 * kernel_scale) * distance + kernel_scale)


def solve_kernel(
    rows,
    cols,
    halo,
    data_in,
    picked,
    core,
    sol_out,
    res_out,
    data,
    marks,
    column,
    band_high,
    band_low,
    mark_high,
    mark_low,
    own_high,
    own_low,
    core_high,
    core_low,
    near_z,
    z_first,
    z_next,
    r_next,
    q_send,
    q_first,
    q_next,
    part_send,
    part_recv,
    row_send,
    row_recv,
    all_send,
    all_recv,
    halo_send_sem,
    halo_recv_sem,
    mark_send_sem,
    mark_recv_sem,
    q_send_sem,
    q_recv_sem,
    q2_send_sem,
    q2_recv_sem,
    part_send_sem,
    part_recv_sem,
    row_send_sem,
    row_recv_sem,
    all_send_sem,
    all_recv_sem,
):
    r = lax.axis_index("rows")
    c = lax.axis_index("cols")
    width = data.shape[2]
    outs = data.shape[1] - PTS
    near = 2 * halo + 1
    piece = 64
    group = outs // cols

    def target(row, col):
        return (row, col)

    def col_peer(step):
        return lax.rem(c + step, cols)

    def row_peer(step):
        return lax.rem(r + step, rows)

    def loop(count, fn, start=0):
        def step(i, carry):
            fn(i)
            return carry

        lax.fori_loop(start, count, step, 0)

    def edge_peers(fn):
        def one(k):
            @pl.when((r < rows - 1) & (k <= c + halo - cols))
            def _():
                fn(k, r + 1, k, halo + cols + k)

            @pl.when((r > 0) & (k >= c))
            def _():
                fn(halo + k, r - 1, cols - halo + k, k)

        loop(halo, one)

    barrier = pltpu.get_barrier_semaphore()

    def greet(row, col):
        pl.semaphore_signal(barrier, inc=1, device_id=target(row, col), device_id_type=MESH)

    loop(cols, lambda i: greet(r, col_peer(i)), 1)
    loop(rows, lambda i: greet(row_peer(i), c), 1)
    edge_peers(lambda index, row, col, slot: greet(row, col))
    right_extra = jnp.where(r < rows - 1, jnp.maximum(c + halo - cols + 1, 0), 0)
    left_extra = jnp.where(r > 0, jnp.maximum(halo - c, 0), 0)
    pl.semaphore_wait(barrier, cols + rows - 2 + right_extra + left_extra)

    def halo_right():
        return pltpu.make_async_remote_copy(
            src_ref=data_in.at[pl.ds(cols - halo, halo)],
            dst_ref=data.at[pl.ds(0, halo)],
            send_sem=halo_send_sem.at[0],
            recv_sem=halo_recv_sem.at[0],
            device_id=target(jnp.minimum(r + 1, rows - 1), c),
            device_id_type=MESH,
        )

    def halo_left():
        return pltpu.make_async_remote_copy(
            src_ref=data_in.at[pl.ds(0, halo)],
            dst_ref=data.at[pl.ds(halo + cols, halo)],
            send_sem=halo_send_sem.at[1],
            recv_sem=halo_recv_sem.at[1],
            device_id=target(jnp.maximum(r - 1, 0), c),
            device_id_type=MESH,
        )

    def mark_copy(peer, slot):
        return pltpu.make_async_remote_copy(
            src_ref=picked,
            dst_ref=marks.at[slot],
            send_sem=mark_send_sem.at[peer],
            recv_sem=mark_recv_sem.at[slot],
            device_id=target(peer, c),
            device_id_type=MESH,
        )

    loop(rows, lambda i: mark_copy(row_peer(i), r).start(), 1)

    @pl.when(r < rows - 1)
    def _():
        halo_right().start()

    @pl.when(r > 0)
    def _():
        halo_left().start()

    def keep(i):
        data[halo + i] = data_in[i]

    loop(cols, keep)
    marks[r] = picked[...]
    high, low = halves(core[...])
    core_high[...] = high
    core_low[...] = low

    @pl.when(r == 0)
    def _():
        data[0:halo] = jnp.zeros((halo,) + data.shape[1:], F32)

    @pl.when(r == rows - 1)
    def _():
        data[halo + cols : 2 * halo + cols] = jnp.zeros((halo,) + data.shape[1:], F32)

    @pl.when(r > 0)
    def _():
        halo_right().wait_recv()

    @pl.when(r < rows - 1)
    def _():
        halo_left().wait_recv()

    own = c + halo

    def fill(lanes, put):
        def one(i):
            at = pl.multiple_of(i * piece, piece)
            high, low = halves(kernel_rows(column[pl.ds(at, piece), :], lanes))
            put(at, high, low)

        for i in range(width // piece):
            one(i)

    own_lanes = data[own, 0:PTS, :]

    def band_slot(i):
        column[...] = jnp.transpose(data[c + i, 0:PTS, :])

        def put(at, high, low):
            band_high[i, pl.ds(at, piece), :] = high
            band_low[i, pl.ds(at, piece), :] = low

        fill(own_lanes, put)

    loop(near, band_slot)

    loop(rows, lambda i: mark_copy(r, row_peer(i)).wait_recv(), 1)
    mark_lanes = jnp.sum(marks[...], axis=0)
    mark_wide = jnp.concatenate(
        [mark_lanes, jnp.zeros((PTS - mark_lanes.shape[0], width), F32)], axis=0
    )
    column[...] = jnp.transpose(own_lanes)

    def put_own(at, high, low):
        own_high[pl.ds(at, piece), :] = high
        own_low[pl.ds(at, piece), :] = low

    fill(mark_wide, put_own)
    column[...] = jnp.transpose(mark_wide)

    def mark_slot(i):
        def put(at, high, low):
            mark_high[i, pl.ds(at, piece), :] = high
            mark_low[i, pl.ds(at, piece), :] = low

        fill(data[i, 0:PTS, :], put)

    def part_copy(k, peer, slot):
        return pltpu.make_async_remote_copy(
            src_ref=part_send.at[k, peer],
            dst_ref=part_recv.at[k, slot],
            send_sem=part_send_sem.at[peer],
            recv_sem=part_recv_sem.at[k, slot],
            device_id=target(r, peer),
            device_id_type=MESH,
        )

    def row_copy(k, peer, slot):
        return pltpu.make_async_remote_copy(
            src_ref=row_send.at[k],
            dst_ref=row_recv.at[k, slot],
            send_sem=row_send_sem.at[peer],
            recv_sem=row_recv_sem.at[k, slot],
            device_id=target(peer, c),
            device_id_type=MESH,
        )

    def all_copy(k, peer, slot):
        return pltpu.make_async_remote_copy(
            src_ref=all_send.at[k],
            dst_ref=all_recv.at[k, slot],
            send_sem=all_send_sem.at[peer],
            recv_sem=all_recv_sem.at[k, slot],
            device_id=target(r, peer),
            device_id_type=MESH,
        )

    def total(k, value, first_work, second_work, third_work):
        for p in range(cols):
            part_send[k, p] = value[p * group : (p + 1) * group, :]
        loop(cols, lambda i: part_copy(k, col_peer(i), c).start(), 1)
        part_recv[k, c] = part_send[k, c]
        first_work()
        loop(cols, lambda i: part_copy(k, c, col_peer(i)).wait_recv(), 1)
        row_part = jnp.sum(part_recv[k], axis=0)
        row_send[k] = row_part
        row_recv[k, r] = row_part
        loop(rows, lambda i: row_copy(k, row_peer(i), r).start(), 1)
        second_work()
        loop(rows, lambda i: row_copy(k, r, row_peer(i)).wait_recv(), 1)
        whole = jnp.sum(row_recv[k], axis=0)
        all_send[k] = whole
        all_recv[k, c] = whole
        loop(cols, lambda i: all_copy(k, col_peer(i), c).start(), 1)
        third_work()
        loop(cols, lambda i: all_copy(k, c, col_peer(i)).wait_recv(), 1)
        loop(cols, lambda i: part_copy(k, col_peer(i), c).wait_send(), 1)
        loop(rows, lambda i: row_copy(k, row_peer(i), r).wait_send(), 1)
        loop(cols, lambda i: all_copy(k, col_peer(i), c).wait_send(), 1)
        return jnp.concatenate([all_recv[k, p] for p in range(cols)], axis=0)

    def message(body, scalars):
        lane = lax.broadcasted_iota(jnp.int32, (outs, 128), 1)
        tail = jnp.zeros((outs, 128), F32)
        for index, scalar in enumerate(scalars):
            tail = jnp.where(lane == index, scalar, tail)
        return jnp.concatenate([body, tail], axis=1)

    def dots(first, second):
        return jnp.sum(first * second, axis=1, keepdims=True)

    def nothing():
        pass

    slots = cols + 2 * halo
    cut_first = slots // 3
    cut_second = (2 * slots) // 3

    own_targets = data[own, PTS:, :]
    sums = total(
        0,
        message(
            product(own_targets, own_high[...], own_low[...]), [dots(own_targets, own_targets)]
        ),
        lambda: loop(cut_first, mark_slot),
        lambda: loop(cut_second, mark_slot, cut_first),
        lambda: loop(slots, mark_slot, cut_second),
    )
    u0 = sums[:, :width]
    w0 = product(u0, core_high[...], core_low[...])
    rz0 = sums[:, width : width + 1] - dots(w0, u0)

    def apply_near(make):
        def step(i, running):
            slot = c + i
            place = r * cols + slot - halo
            valid = (place >= 0) & (place < rows * cols)
            value = jnp.where(valid, make(slot), 0.0)
            near_z[i] = value
            return running + product(value, band_high[i], band_low[i])

        image = lax.fori_loop(0, near, step, jnp.zeros((outs, width), F32))
        return image + ridge_shift * near_z[halo]

    def first_z(slot):
        return data[slot, PTS:, :] - product(w0, mark_high[slot], mark_low[slot])

    q0 = apply_near(first_z)
    z0_own = near_z[halo]
    q_send[0] = q0
    q_first[own] = q0

    def q_copy(index, row, col, slot):
        return pltpu.make_async_remote_copy(
            src_ref=q_send.at[0],
            dst_ref=q_first.at[slot],
            send_sem=q_send_sem.at[index],
            recv_sem=q_recv_sem.at[slot],
            device_id=target(row, col),
            device_id_type=MESH,
        )

    def send_index(peer):
        return 2 * halo + peer

    image_message = message(product(q0, own_high[...], own_low[...]), [dots(z0_own, q0)])

    def send_first():
        edge_peers(
            lambda index, row, col, slot: q_copy(
                index, row, col, jnp.where(row > r, c - cols + halo, halo + cols + c)
            ).start()
        )
        loop(cols, lambda i: q_copy(send_index(col_peer(i)), r, col_peer(i), own).start(), 1)

    def first_slab(i):
        z_first[i] = first_z(halo + i)

    def take_first():
        edge_peers(lambda index, row, col, slot: q_copy(index, row, col, slot).wait_recv())
        loop(
            cols,
            lambda i: q_copy(send_index(c), r, c, halo + col_peer(i)).wait_recv(),
            1,
        )

    sums = total(
        1, image_message, send_first, lambda: loop(cols, first_slab), take_first
    )
    edge_peers(lambda index, row, col, slot: q_copy(index, row, col, slot).wait_send())
    loop(cols, lambda i: q_copy(send_index(col_peer(i)), r, col_peer(i), own).wait_send(), 1)

    curve0 = sums[:, width : width + 1]
    alpha0 = rz0 / curve0
    u1 = u0 - alpha0 * sums[:, :width]
    w1 = product(u1, core_high[...], core_low[...])

    def next_r(slot):
        return data[slot, PTS:, :] - alpha0 * q_first[slot]

    def next_z(slot):
        return next_r(slot) - product(w1, mark_high[slot], mark_low[slot])

    image = apply_near(next_z)
    z1_own = near_z[halo]
    r1_own = next_r(own)
    q_send[1] = image
    q_next[c] = image

    def q2_copy(peer, slot):
        return pltpu.make_async_remote_copy(
            src_ref=q_send.at[1],
            dst_ref=q_next.at[slot],
            send_sem=q2_send_sem.at[peer],
            recv_sem=q2_recv_sem.at[slot],
            device_id=target(r, peer),
            device_id_type=MESH,
        )

    def next_slab(i):
        residual = next_r(halo + i)
        r_next[i] = residual
        z_next[i] = residual - product(w1, mark_high[halo + i], mark_low[halo + i])

    sums = total(
        2,
        message(
            jnp.zeros((outs, width), F32),
            [dots(r1_own, z1_own), dots(z1_own, image), dots(z1_own, q0) + dots(z0_own, image)],
        ),
        lambda: loop(cols, lambda i: q2_copy(col_peer(i), c).start(), 1),
        lambda: loop(cols, next_slab),
        lambda: loop(cols, lambda i: q2_copy(c, col_peer(i)).wait_recv(), 1),
    )
    rz1 = sums[:, width : width + 1]
    beta = rz1 / rz0
    curve1 = sums[:, width + 1 : width + 2] + beta * (
        sums[:, width + 2 : width + 3] + beta * curve0
    )
    alpha1 = rz1 / curve1

    def finish(i):
        at = pl.ds(pl.multiple_of(i * width, width), width)
        first = z_first[i]
        sol_out[:, at] = alpha0 * first + alpha1 * (z_next[i] + beta * first)
        res_out[:, at] = r_next[i] - alpha1 * (q_next[i] + beta * q_first[halo + i])

    loop(cols, finish)

    loop(cols, lambda i: q2_copy(col_peer(i), c).wait_send(), 1)
    loop(rows, lambda i: mark_copy(row_peer(i), r).wait_send(), 1)

    @pl.when(r < rows - 1)
    def _():
        halo_right().wait_send()

    @pl.when(r > 0)
    def _():
        halo_left().wait_send()


def body(points, targets, landmarks, neighbours, counts, core_inverse):
    cols = lax.axis_size("cols")
    rows = lax.axis_size("rows")
    row_index = lax.axis_index("rows")
    slab = points.shape[1]
    block = slab // neighbours.shape[0]
    width = slab // cols
    outs = targets.shape[0]
    land = landmarks.shape[0]
    halo = -(-REACH * block // width)
    near = 2 * halo + 1
    slots = cols + 2 * halo

    local_ids = landmarks - row_index * slab
    present = (local_ids >= 0) & (local_ids < slab)
    picked = jnp.take(points, jnp.clip(local_ids, 0, slab - 1), axis=1)
    picked = jnp.where(present[None, :], picked, 0.0)
    picked = jnp.concatenate([picked, jnp.zeros((1, land), F32)], axis=0)
    lines = PTS + outs
    data = jnp.concatenate([points, jnp.zeros((PTS - 3, slab), F32), targets], axis=0)
    data = data.reshape(lines, cols, width).transpose(1, 0, 2)

    vmem = pltpu.VMEM
    dma = pltpu.SemaphoreType.DMA
    group = outs // cols
    wide = land + 128
    scratch = [
        vmem((slots, lines, width), F32),
        vmem((rows, 4, land), F32),
        vmem((width, PTS), F32),
        vmem((near, width, width), BF16),
        vmem((near, width, width), BF16),
        vmem((slots, land, width), BF16),
        vmem((slots, land, width), BF16),
        vmem((width, land), BF16),
        vmem((width, land), BF16),
        vmem((land, land), BF16),
        vmem((land, land), BF16),
        vmem((near, outs, width), F32),
        vmem((cols, outs, width), F32),
        vmem((cols, outs, width), F32),
        vmem((cols, outs, width), F32),
        vmem((2, outs, width), F32),
        vmem((slots, outs, width), F32),
        vmem((cols, outs, width), F32),
        vmem((3, cols, group, wide), F32),
        vmem((3, cols, group, wide), F32),
        vmem((3, group, wide), F32),
        vmem((3, rows, group, wide), F32),
        vmem((3, group, wide), F32),
        vmem((3, cols, group, wide), F32),
        dma((2,)),
        dma((2,)),
        dma((rows,)),
        dma((rows,)),
        dma((slots,)),
        dma((slots,)),
        dma((cols,)),
        dma((cols,)),
        dma((cols,)),
        dma((3, cols)),
        dma((rows,)),
        dma((3, rows)),
        dma((cols,)),
        dma((3, cols)),
    ]
    shape = jax.ShapeDtypeStruct((outs, slab), F32)
    return tuple(
        pl.pallas_call(
            functools.partial(solve_kernel, rows, cols, halo),
            out_shape=(shape, shape),
            in_specs=[pl.BlockSpec(memory_space=pltpu.VMEM)] * 3,
            out_specs=[pl.BlockSpec(memory_space=pltpu.VMEM)] * 2,
            scratch_shapes=scratch,
            compiler_params=pltpu.CompilerParams(
                collective_id=0,
                has_side_effects=True,
                vmem_limit_bytes=48 * 1024 * 1024,
            ),
        )(data, picked, core_inverse)
    )


def solution(mesh):
    placed = (P(None, "rows"), P(None, "rows"), P(), P("rows", None), P("rows"), P())
    return jax.shard_map(
        body,
        mesh=mesh,
        in_specs=placed,
        out_specs=(P(None, "rows"), P(None, "rows")),
        check_vma=False,
    )
```

time: 355 us -> 100 us (0.28); the launches traced: 348 us -> 100 us
  blocking collectives: 281 us -> 0 us
  Pallas kernels: 0 us -> 94.8 us
  matrix products: 38.9 us -> 0 us
  other arithmetic: 12.2 us -> 0.86 us
  starting transfers between devices: 9.29 us -> 0 us
    all_gather x9 -> x0, blocking collectives: 281 us -> none  [the longest x3 112 us: total(): return jnp.sum(lax.all_gather(part, 'rows'), axis=0)]
    pallas_call x0 -> x1, Pallas kernels: none -> 94.8 us  [body(): pl.pallas_call(functools.partial(solve_kernel, rows, cols, halo), out_sha...]
    dot_general x8 -> x0, matrix products: 38.9 us -> none  [product(): return jnp.dot(first, second, precision=lax.Precision.HIGHEST)]
    ppermute x4 -> x0, starting transfers between devices: 9.29 us -> none  [the longest x2 6.7 us: extended(): lax.ppermute(tail, 'rows', [(i, i + 1) for i in range(count - 1)])]
    mul x1 -> x0, other arithmetic: 5.62 us -> none  [body(): marks_wide = kernel_scale * kernel_matrix(marks, wide_points)]
  transfers between devices with their start and end apart: 4 -> 0, of which waited for: 0 -> 0; matrix products, arithmetic and copies ran while one was open for 1% -> 0% of each run, Pallas kernels for 0% -> 0%
where the time goes in v2:
time: 100 us
  Pallas kernels  94.8 us (95%)
  local copies, waits for them, and re-layouts  3.82 us (4%)
    pallas_call x1, Pallas kernels, body(): pl.pallas_call(functools.partial(solve_kernel, rows, cols, halo), out_sha...  94.8 us
    unnamed x9, local copies, waits for them, and re-layouts  2.89 us

profile of v2, /device:TPU:1, one launch (start us, length us, event | category | flops | bytes accessed | tf_op | source)
XLA Modules:
  0.0 100.2 jit_solution(9102465736579724716)
XLA Ops:
  0.6 0.0 copy-start.1
  0.6 0.0 copy-start.2
  0.7 0.0 copy-start
  0.7 0.7 compare_and_fusion
  1.4 1.5 %copy.9 = f32[3,4096]{0,1:T(8,128)S(1)} copy(f32[3,4096]{1,0:T(4,128)} %param.6) | data formatting | bytes 98304 | tf_op args[0]
  2.9 0.7 gather_fusion
  3.6 0.1 copy.10
  3.8 0.1 pad.2.clone
  3.8 0.0 copy-done.1
  3.8 0.0 copy-done.2
  3.8 0.1 pad_maximum_fusion
  4.0 0.0 copy-done
  4.0 94.8 %shard_map.59 = (f32[16,4096]{1,0:T(8,128)S(1)}, f32[16,4096]{1,0:T(8,128)S(1)}) custom-call(f32[16,24,256]{2,1,0:T(8,128)S(1)} %bitcast.9, f32[4,256]{1,0:T(4,128)S(1)} %concatenate.7.picked, f32[256,256]{1,0:T(8,128)S(1)} %copy-done), custom_call_target="tpu_custom_call" | custom-call | tf_op jit(solution)/shard_map/pallas_call | solution.py:536
  98.7 0.7 copy.16
  99.5 0.7 copy.17
  (5 shorter events, 0.1 us)
Async XLA Ops:
  0.6 3.2 %copy-start.1 = (f32[3,4096]{1,0:T(4,128)S(1)}, f32[3,4096]{1,0:T(4,128)}, u32[]{:S(2)}) copy-start(f32[3,4096]{1,0:T(4,128)} %param.6) | copy-start | bytes 147460
  0.6 3.2 %copy-start.2 = (f32[16,4096]{1,0:T(8,128)S(1)}, f32[16,4096]{1,0:T(8,128)}, u32[]{:S(2)}) copy-start(f32[16,4096]{1,0:T(8,128)} %param.7) | copy-start | bytes 786436
  0.7 3.3 %copy-start = (f32[256,256]{1,0:T(8,128)S(1)}, f32[256,256]{1,0:T(8,128)}, u32[]{:S(2)}) copy-start(f32[256,256]{1,0:T(8,128)} %core.1) | copy-start | bytes 786436

commit v3 on v2

--- a/solution.py
+++ b/solution.py
@@ -51,6 +51,7 @@
     halo,
     data_in,
     picked,
+    close,
     core,
     sol_out,
     res_out,
@@ -78,6 +79,10 @@
     row_recv,
     all_send,
     all_recv,
+    small_send,
+    small_recv,
+    last_send,
+    last_recv,
     halo_send_sem,
     halo_recv_sem,
     mark_send_sem,
@@ -171,7 +176,9 @@
             device_id_type=MESH,
         )
 
-    loop(rows, lambda i: mark_copy(row_peer(i), r).start(), 1)
+    mark_copy(row_peer(1), r).start()
+    mark_copy(row_peer(rows - 1), r).start()
+    loop(rows - 1, lambda i: mark_copy(row_peer(i), r).start(), 2)
 
     @pl.when(r < rows - 1)
     def _():
@@ -198,14 +205,6 @@
     def _():
         data[halo + cols : 2 * halo + cols] = jnp.zeros((halo,) + data.shape[1:], F32)
 
-    @pl.when(r > 0)
-    def _():
-        halo_right().wait_recv()
-
-    @pl.when(r < rows - 1)
-    def _():
-        halo_left().wait_recv()
-
     own = c + halo
 
     def fill(lanes, put):
@@ -217,7 +216,7 @@
         for i in range(width // piece):
             one(i)
 
-    own_lanes = data[own, 0:PTS, :]
+    own_lanes = data_in[c, 0:PTS, :]
 
     def band_slot(i):
         column[...] = jnp.transpose(data[c + i, 0:PTS, :])
@@ -228,21 +227,24 @@
 
         fill(own_lanes, put)
 
-    loop(near, band_slot)
-
-    loop(rows, lambda i: mark_copy(r, row_peer(i)).wait_recv(), 1)
-    mark_lanes = jnp.sum(marks[...], axis=0)
-    mark_wide = jnp.concatenate(
-        [mark_lanes, jnp.zeros((PTS - mark_lanes.shape[0], width), F32)], axis=0
-    )
+    def widen(lanes):
+        return jnp.concatenate([lanes, jnp.zeros((PTS - lanes.shape[0], width), F32)], axis=0)
+
+    before = row_peer(rows - 1)
+    after = row_peer(1)
+    mark_copy(r, before).wait_recv()
+    mark_copy(r, after).wait_recv()
+    close_lanes = widen(marks[before] + picked[...] + marks[after])
     column[...] = jnp.transpose(own_lanes)
+    close_row = close[0:1, :]
 
     def put_own(at, high, low):
+        high = high * close_row.astype(BF16)
+        low = low * close_row.astype(BF16)
         own_high[pl.ds(at, piece), :] = high
         own_low[pl.ds(at, piece), :] = low
 
-    fill(mark_wide, put_own)
-    column[...] = jnp.transpose(mark_wide)
+    fill(close_lanes, put_own)
 
     def mark_slot(i):
         def put(at, high, low):
@@ -250,6 +252,22 @@
             mark_low[i, pl.ds(at, piece), :] = low
 
         fill(data[i, 0:PTS, :], put)
+
+    def first_band():
+        @pl.when(r > 0)
+        def _():
+            halo_right().wait_recv()
+
+        @pl.when(r < rows - 1)
+        def _():
+            halo_left().wait_recv()
+
+        loop(near, band_slot)
+
+    def first_marks():
+        loop(rows - 1, lambda i: mark_copy(r, row_peer(i)).wait_recv(), 2)
+        column[...] = jnp.transpose(widen(jnp.sum(marks[...], axis=0)))
+        loop(near, lambda i: mark_slot(c + i))
 
     def part_copy(k, peer, slot):
         return pltpu.make_async_remote_copy(
@@ -319,18 +337,16 @@
         pass
 
     slots = cols + 2 * halo
-    cut_first = slots // 3
-    cut_second = (2 * slots) // 3
-
-    own_targets = data[own, PTS:, :]
+
+    own_targets = data_in[c, PTS:, :]
     sums = total(
         0,
         message(
             product(own_targets, own_high[...], own_low[...]), [dots(own_targets, own_targets)]
         ),
-        lambda: loop(cut_first, mark_slot),
-        lambda: loop(cut_second, mark_slot, cut_first),
-        lambda: loop(slots, mark_slot, cut_second),
+        first_band,
+        first_marks,
+        nothing,
     )
     u0 = sums[:, :width]
     w0 = product(u0, core_high[...], core_low[...])
@@ -378,6 +394,7 @@
             ).start()
         )
         loop(cols, lambda i: q_copy(send_index(col_peer(i)), r, col_peer(i), own).start(), 1)
+        loop(slots - near, lambda i: mark_slot(lax.rem(c + near + i, slots)))
 
     def first_slab(i):
         z_first[i] = first_z(halo + i)
@@ -428,21 +445,57 @@
         r_next[i] = residual
         z_next[i] = residual - product(w1, mark_high[halo + i], mark_low[halo + i])
 
-    sums = total(
-        2,
-        message(
-            jnp.zeros((outs, width), F32),
-            [dots(r1_own, z1_own), dots(z1_own, image), dots(z1_own, q0) + dots(z0_own, image)],
-        ),
-        lambda: loop(cols, lambda i: q2_copy(col_peer(i), c).start(), 1),
-        lambda: loop(cols, next_slab),
-        lambda: loop(cols, lambda i: q2_copy(c, col_peer(i)).wait_recv(), 1),
-    )
-    rz1 = sums[:, width : width + 1]
+    lane = lax.broadcasted_iota(jnp.int32, (outs, 128), 1)
+    line = lax.broadcasted_iota(jnp.int32, (outs, 128), 0)
+
+    def small_copy(peer, slot):
+        return pltpu.make_async_remote_copy(
+            src_ref=small_send,
+            dst_ref=small_recv.at[slot],
+            send_sem=part_send_sem.at[peer],
+            recv_sem=part_recv_sem.at[2, slot],
+            device_id=target(r, peer),
+            device_id_type=MESH,
+        )
+
+    def last_copy(peer, slot):
+        return pltpu.make_async_remote_copy(
+            src_ref=last_send,
+            dst_ref=last_recv.at[slot],
+            send_sem=row_send_sem.at[peer],
+            recv_sem=row_recv_sem.at[2, slot],
+            device_id=target(peer, c),
+            device_id_type=MESH,
+        )
+
+    packed = jnp.zeros((outs, 128), F32)
+    for index, scalar in enumerate(
+        [dots(r1_own, z1_own), dots(z1_own, image), dots(z1_own, q0) + dots(z0_own, image)]
+    ):
+        packed = jnp.where(lane == line + index * outs, scalar, packed)
+    packed = jnp.sum(packed, axis=0, keepdims=True)
+    small_send[...] = packed
+    small_recv[c] = packed
+    loop(cols, lambda i: small_copy(col_peer(i), c).start(), 1)
+    loop(cols, lambda i: q2_copy(col_peer(i), c).start(), 1)
+    loop(cols // 2, next_slab)
+    loop(cols, lambda i: small_copy(c, col_peer(i)).wait_recv(), 1)
+    packed = jnp.sum(small_recv[...], axis=0)
+    last_send[...] = packed
+    last_recv[r] = packed
+    loop(rows, lambda i: last_copy(row_peer(i), r).start(), 1)
+    loop(cols, next_slab, cols // 2)
+    loop(cols, lambda i: q2_copy(c, col_peer(i)).wait_recv(), 1)
+    loop(rows, lambda i: last_copy(r, row_peer(i)).wait_recv(), 1)
+    whole = jnp.sum(last_recv[...], axis=0)
+
+    def taken(index):
+        picked_lane = jnp.where(lane == line + index * outs, whole, 0.0)
+        return jnp.sum(picked_lane, axis=1, keepdims=True)
+
+    rz1 = taken(0)
     beta = rz1 / rz0
-    curve1 = sums[:, width + 1 : width + 2] + beta * (
-        sums[:, width + 2 : width + 3] + beta * curve0
-    )
+    curve1 = taken(1) + beta * (taken(2) + beta * curve0)
     alpha1 = rz1 / curve1
 
     def finish(i):
@@ -453,6 +506,8 @@
 
     loop(cols, finish)
 
+    loop(cols, lambda i: small_copy(col_peer(i), c).wait_send(), 1)
+    loop(rows, lambda i: last_copy(row_peer(i), r).wait_send(), 1)
     loop(cols, lambda i: q2_copy(col_peer(i), c).wait_send(), 1)
     loop(rows, lambda i: mark_copy(row_peer(i), r).wait_send(), 1)
 
@@ -483,6 +538,8 @@
     picked = jnp.take(points, jnp.clip(local_ids, 0, slab - 1), axis=1)
     picked = jnp.where(present[None, :], picked, 0.0)
     picked = jnp.concatenate([picked, jnp.zeros((1, land), F32)], axis=0)
+    close = (local_ids >= -slab) & (local_ids < 2 * slab)
+    close = jnp.broadcast_to(close[None, :].astype(F32), (8, land))
     lines = PTS + outs
     data = jnp.concatenate([points, jnp.zeros((PTS - 3, slab), F32), targets], axis=0)
     data = data.reshape(lines, cols, width).transpose(1, 0, 2)
@@ -510,12 +567,16 @@
         vmem((2, outs, width), F32),
         vmem((slots, outs, width), F32),
         vmem((cols, outs, width), F32),
-        vmem((3, cols, group, wide), F32),
-        vmem((3, cols, group, wide), F32),
-        vmem((3, group, wide), F32),
-        vmem((3, rows, group, wide), F32),
-        vmem((3, group, wide), F32),
-        vmem((3, cols, group, wide), F32),
+        vmem((2, cols, group, wide), F32),
+        vmem((2, cols, group, wide), F32),
+        vmem((2, group, wide), F32),
+        vmem((2, rows, group, wide), F32),
+        vmem((2, group, wide), F32),
+        vmem((2, cols, group, wide), F32),
+        vmem((1, 128), F32),
+        vmem((cols, 1, 128), F32),
+        vmem((1, 128), F32),
+        vmem((rows, 1, 128), F32),
         dma((2,)),
         dma((2,)),
         dma((rows,)),
@@ -529,14 +590,14 @@
         dma((rows,)),
         dma((3, rows)),
         dma((cols,)),
-        dma((3, cols)),
+        dma((2, cols)),
     ]
     shape = jax.ShapeDtypeStruct((outs, slab), F32)
     return tuple(
         pl.pallas_call(
             functools.partial(solve_kernel, rows, cols, halo),
             out_shape=(shape, shape),
-            in_specs=[pl.BlockSpec(memory_space=pltpu.VMEM)] * 3,
+            in_specs=[pl.BlockSpec(memory_space=pltpu.VMEM)] * 4,
             out_specs=[pl.BlockSpec(memory_space=pltpu.VMEM)] * 2,
             scratch_shapes=scratch,
             compiler_params=pltpu.CompilerParams(
@@ -544,7 +605,7 @@
                 has_side_effects=True,
                 vmem_limit_bytes=48 * 1024 * 1024,
             ),
-        )(data, picked, core_inverse)
+        )(data, picked, close, core_inverse)
     )
 
 

time: 100 us -> 89.3 us (0.89)
  Pallas kernels: 94.8 us -> 83.7 us
    pallas_call x1, Pallas kernels: 94.8 us -> 83.7 us  [body(): pl.pallas_call(functools.partial(solve_kernel, rows, cols, halo), out_sha...]
where the time goes in v3:
time: 89.3 us; the launch traced here: 89.1 us
  Pallas kernels  83.7 us (94%)
  local copies, waits for them, and re-layouts  3.82 us (4%)
    pallas_call x1, Pallas kernels, body(): pl.pallas_call(functools.partial(solve_kernel, rows, cols, halo), out_sha...  83.7 us
    unnamed x9, local copies, waits for them, and re-layouts  2.89 us

profile of v3, /device:TPU:1, one launch (start us, length us, event | category | flops | bytes accessed | tf_op | source)
XLA Modules:
  0.0 89.1 jit_solution(17198519604137677053)
XLA Ops:
  0.6 0.0 copy-start.1
  0.6 0.0 copy-start.2
  0.7 0.0 copy-start
  0.7 0.7 and_convert_fusion
  1.4 1.5 %copy.9 = f32[3,4096]{0,1:T(8,128)S(1)} copy(f32[3,4096]{1,0:T(4,128)} %param.6) | data formatting | bytes 98304 | tf_op args[0]
  2.9 0.7 gather_fusion
  3.6 0.1 copy.10
  3.8 0.1 pad.2.clone
  3.8 0.0 copy-done.1
  3.8 0.0 copy-done.2
  3.8 0.1 pad_maximum_fusion
  4.0 0.0 copy-done
  4.0 83.7 %shard_map.59 = (f32[16,4096]{1,0:T(8,128)S(1)}, f32[16,4096]{1,0:T(8,128)S(1)}) custom-call(f32[16,24,256]{2,1,0:T(8,128)S(1)} %bitcast.9, f32[4,256]{1,0:T(4,128)S(1)} %concatenate.7.picked, f32[8,256]{1,0:T(8,128)S(1)} %broadcast_in_dim.41.close, f32[256,256]{1,0:T(8,128)S(1)} %copy-done), custom_call_target="tpu_custom_call" | custom-call | tf_op jit(solution)/shard_map/pallas_call | solution.py:597
  87.7 0.7 copy.16
  88.4 0.7 copy.17
  (6 shorter events, 0.1 us)
Async XLA Ops:
  0.6 3.2 %copy-start.1 = (f32[3,4096]{1,0:T(4,128)S(1)}, f32[3,4096]{1,0:T(4,128)}, u32[]{:S(2)}) copy-start(f32[3,4096]{1,0:T(4,128)} %param.6) | copy-start | bytes 147460
  0.6 3.2 %copy-start.2 = (f32[16,4096]{1,0:T(8,128)S(1)}, f32[16,4096]{1,0:T(8,128)}, u32[]{:S(2)}) copy-start(f32[16,4096]{1,0:T(8,128)} %param.7) | copy-start | bytes 786436
  0.7 3.3 %copy-start = (f32[256,256]{1,0:T(8,128)S(1)}, f32[256,256]{1,0:T(8,128)}, u32[]{:S(2)}) copy-start(f32[256,256]{1,0:T(8,128)} %core.1) | copy-start | bytes 786436

commit v4 on v3

--- a/solution.py
+++ b/solution.py
@@ -134,6 +134,16 @@
 
         loop(halo, one)
 
+    def bulk(ref, send_sem, recv_sem):
+        return pltpu.make_async_remote_copy(
+            src_ref=ref,
+            dst_ref=ref,
+            send_sem=send_sem,
+            recv_sem=recv_sem,
+            device_id=target(r, c),
+            device_id_type=MESH,
+        )
+
     barrier = pltpu.get_barrier_semaphore()
 
     def greet(row, col):
@@ -166,18 +176,18 @@
             device_id_type=MESH,
         )
 
-    def mark_copy(peer, slot):
+    def mark_copy(peer, slot, sem=2):
         return pltpu.make_async_remote_copy(
             src_ref=picked,
             dst_ref=marks.at[slot],
-            send_sem=mark_send_sem.at[peer],
-            recv_sem=mark_recv_sem.at[slot],
+            send_sem=mark_send_sem.at[sem],
+            recv_sem=mark_recv_sem.at[sem],
             device_id=target(peer, c),
             device_id_type=MESH,
         )
 
-    mark_copy(row_peer(1), r).start()
-    mark_copy(row_peer(rows - 1), r).start()
+    mark_copy(row_peer(1), r, 0).start()
+    mark_copy(row_peer(rows - 1), r, 1).start()
     loop(rows - 1, lambda i: mark_copy(row_peer(i), r).start(), 2)
 
     @pl.when(r < rows - 1)
@@ -232,8 +242,8 @@
 
     before = row_peer(rows - 1)
     after = row_peer(1)
-    mark_copy(r, before).wait_recv()
-    mark_copy(r, after).wait_recv()
+    mark_copy(r, before, 0).wait_recv()
+    mark_copy(r, after, 1).wait_recv()
     close_lanes = widen(marks[before] + picked[...] + marks[after])
     column[...] = jnp.transpose(own_lanes)
     close_row = close[0:1, :]
@@ -264,8 +274,11 @@
 
         loop(near, band_slot)
 
+    def marks_done():
+        return bulk(marks.at[pl.ds(0, rows - 3)], mark_send_sem.at[2], mark_recv_sem.at[2])
+
     def first_marks():
-        loop(rows - 1, lambda i: mark_copy(r, row_peer(i)).wait_recv(), 2)
+        marks_done().wait_recv()
         column[...] = jnp.transpose(widen(jnp.sum(marks[...], axis=0)))
         loop(near, lambda i: mark_slot(c + i))
 
@@ -273,8 +286,8 @@
         return pltpu.make_async_remote_copy(
             src_ref=part_send.at[k, peer],
             dst_ref=part_recv.at[k, slot],
-            send_sem=part_send_sem.at[peer],
-            recv_sem=part_recv_sem.at[k, slot],
+            send_sem=part_send_sem.at[k],
+            recv_sem=part_recv_sem.at[k],
             device_id=target(r, peer),
             device_id_type=MESH,
         )
@@ -283,8 +296,8 @@
         return pltpu.make_async_remote_copy(
             src_ref=row_send.at[k],
             dst_ref=row_recv.at[k, slot],
-            send_sem=row_send_sem.at[peer],
-            recv_sem=row_recv_sem.at[k, slot],
+            send_sem=row_send_sem.at[k],
+            recv_sem=row_recv_sem.at[k],
             device_id=target(peer, c),
             device_id_type=MESH,
         )
@@ -293,11 +306,20 @@
         return pltpu.make_async_remote_copy(
             src_ref=all_send.at[k],
             dst_ref=all_recv.at[k, slot],
-            send_sem=all_send_sem.at[peer],
-            recv_sem=all_recv_sem.at[k, slot],
+            send_sem=all_send_sem.at[k],
+            recv_sem=all_recv_sem.at[k],
             device_id=target(r, peer),
             device_id_type=MESH,
         )
+
+    def part_done(k):
+        return bulk(part_recv.at[k, pl.ds(0, cols - 1)], part_send_sem.at[k], part_recv_sem.at[k])
+
+    def row_done(k):
+        return bulk(row_recv.at[k, pl.ds(0, rows - 1)], row_send_sem.at[k], row_recv_sem.at[k])
+
+    def all_done(k):
+        return bulk(all_recv.at[k, pl.ds(0, cols - 1)], all_send_sem.at[k], all_recv_sem.at[k])
 
     def total(k, value, first_work, second_work, third_work):
         for p in range(cols):
@@ -305,22 +327,19 @@
         loop(cols, lambda i: part_copy(k, col_peer(i), c).start(), 1)
         part_recv[k, c] = part_send[k, c]
         first_work()
-        loop(cols, lambda i: part_copy(k, c, col_peer(i)).wait_recv(), 1)
+        part_done(k).wait_recv()
         row_part = jnp.sum(part_recv[k], axis=0)
         row_send[k] = row_part
         row_recv[k, r] = row_part
         loop(rows, lambda i: row_copy(k, row_peer(i), r).start(), 1)
         second_work()
-        loop(rows, lambda i: row_copy(k, r, row_peer(i)).wait_recv(), 1)
+        row_done(k).wait_recv()
         whole = jnp.sum(row_recv[k], axis=0)
         all_send[k] = whole
         all_recv[k, c] = whole
         loop(cols, lambda i: all_copy(k, col_peer(i), c).start(), 1)
         third_work()
-        loop(cols, lambda i: all_copy(k, c, col_peer(i)).wait_recv(), 1)
-        loop(cols, lambda i: part_copy(k, col_peer(i), c).wait_send(), 1)
-        loop(rows, lambda i: row_copy(k, row_peer(i), r).wait_send(), 1)
-        loop(cols, lambda i: all_copy(k, col_peer(i), c).wait_send(), 1)
+        all_done(k).wait_recv()
         return jnp.concatenate([all_recv[k, p] for p in range(cols)], axis=0)
 
     def message(body, scalars):
@@ -372,18 +391,18 @@
     q_send[0] = q0
     q_first[own] = q0
 
-    def q_copy(index, row, col, slot):
+    def q_copy(index, row, col, slot, sem=None):
         return pltpu.make_async_remote_copy(
             src_ref=q_send.at[0],
             dst_ref=q_first.at[slot],
             send_sem=q_send_sem.at[index],
-            recv_sem=q_recv_sem.at[slot],
+            recv_sem=q_recv_sem.at[slot if sem is None else sem],
             device_id=target(row, col),
             device_id_type=MESH,
         )
 
-    def send_index(peer):
-        return 2 * halo + peer
+    def q_done():
+        return bulk(q_first.at[pl.ds(0, cols - 1)], q_send_sem.at[slots], q_recv_sem.at[slots])
 
     image_message = message(product(q0, own_high[...], own_low[...]), [dots(z0_own, q0)])
 
@@ -393,7 +412,7 @@
                 index, row, col, jnp.where(row > r, c - cols + halo, halo + cols + c)
             ).start()
         )
-        loop(cols, lambda i: q_copy(send_index(col_peer(i)), r, col_peer(i), own).start(), 1)
+        loop(cols, lambda i: q_copy(slots, r, col_peer(i), own, slots).start(), 1)
         loop(slots - near, lambda i: mark_slot(lax.rem(c + near + i, slots)))
 
     def first_slab(i):
@@ -401,17 +420,11 @@
 
     def take_first():
         edge_peers(lambda index, row, col, slot: q_copy(index, row, col, slot).wait_recv())
-        loop(
-            cols,
-            lambda i: q_copy(send_index(c), r, c, halo + col_peer(i)).wait_recv(),
-            1,
-        )
+        q_done().wait_recv()
 
     sums = total(
         1, image_message, send_first, lambda: loop(cols, first_slab), take_first
     )
-    edge_peers(lambda index, row, col, slot: q_copy(index, row, col, slot).wait_send())
-    loop(cols, lambda i: q_copy(send_index(col_peer(i)), r, col_peer(i), own).wait_send(), 1)
 
     curve0 = sums[:, width : width + 1]
     alpha0 = rz0 / curve0
@@ -434,8 +447,8 @@
         return pltpu.make_async_remote_copy(
             src_ref=q_send.at[1],
             dst_ref=q_next.at[slot],
-            send_sem=q2_send_sem.at[peer],
-            recv_sem=q2_recv_sem.at[slot],
+            send_sem=q2_send_sem.at[0],
+            recv_sem=q2_recv_sem.at[0],
             device_id=target(r, peer),
             device_id_type=MESH,
         )
@@ -452,8 +465,8 @@
         return pltpu.make_async_remote_copy(
             src_ref=small_send,
             dst_ref=small_recv.at[slot],
-            send_sem=part_send_sem.at[peer],
-            recv_sem=part_recv_sem.at[2, slot],
+            send_sem=part_send_sem.at[2],
+            recv_sem=part_recv_sem.at[2],
             device_id=target(r, peer),
             device_id_type=MESH,
         )
@@ -462,8 +475,8 @@
         return pltpu.make_async_remote_copy(
             src_ref=last_send,
             dst_ref=last_recv.at[slot],
-            send_sem=row_send_sem.at[peer],
-            recv_sem=row_recv_sem.at[2, slot],
+            send_sem=row_send_sem.at[2],
+            recv_sem=row_recv_sem.at[2],
             device_id=target(peer, c),
             device_id_type=MESH,
         )
@@ -479,14 +492,19 @@
     loop(cols, lambda i: small_copy(col_peer(i), c).start(), 1)
     loop(cols, lambda i: q2_copy(col_peer(i), c).start(), 1)
     loop(cols // 2, next_slab)
-    loop(cols, lambda i: small_copy(c, col_peer(i)).wait_recv(), 1)
+    small_done = bulk(
+        small_recv.at[pl.ds(0, cols - 1)], part_send_sem.at[2], part_recv_sem.at[2]
+    )
+    small_done.wait_recv()
     packed = jnp.sum(small_recv[...], axis=0)
     last_send[...] = packed
     last_recv[r] = packed
     loop(rows, lambda i: last_copy(row_peer(i), r).start(), 1)
     loop(cols, next_slab, cols // 2)
-    loop(cols, lambda i: q2_copy(c, col_peer(i)).wait_recv(), 1)
-    loop(rows, lambda i: last_copy(r, row_peer(i)).wait_recv(), 1)
+    q2_done = bulk(q_next.at[pl.ds(0, cols - 1)], q2_send_sem.at[0], q2_recv_sem.at[0])
+    q2_done.wait_recv()
+    last_done = bulk(last_recv.at[pl.ds(0, rows - 1)], row_send_sem.at[2], row_recv_sem.at[2])
+    last_done.wait_recv()
     whole = jnp.sum(last_recv[...], axis=0)
 
     def taken(index):
@@ -506,10 +524,18 @@
 
     loop(cols, finish)
 
-    loop(cols, lambda i: small_copy(col_peer(i), c).wait_send(), 1)
-    loop(rows, lambda i: last_copy(row_peer(i), r).wait_send(), 1)
-    loop(cols, lambda i: q2_copy(col_peer(i), c).wait_send(), 1)
-    loop(rows, lambda i: mark_copy(row_peer(i), r).wait_send(), 1)
+    for k in range(2):
+        part_done(k).wait_send()
+        row_done(k).wait_send()
+        all_done(k).wait_send()
+    small_done.wait_send()
+    last_done.wait_send()
+    edge_peers(lambda index, row, col, slot: q_copy(index, row, col, slot).wait_send())
+    q_done().wait_send()
+    q2_done.wait_send()
+    mark_copy(row_peer(1), r, 0).wait_send()
+    mark_copy(row_peer(rows - 1), r, 1).wait_send()
+    marks_done().wait_send()
 
     @pl.when(r < rows - 1)
     def _():
@@ -579,18 +605,18 @@
         vmem((rows, 1, 128), F32),
         dma((2,)),
         dma((2,)),
-        dma((rows,)),
-        dma((rows,)),
-        dma((slots,)),
-        dma((slots,)),
-        dma((cols,)),
-        dma((cols,)),
-        dma((cols,)),
-        dma((3, cols)),
-        dma((rows,)),
-        dma((3, rows)),
-        dma((cols,)),
-        dma((2, cols)),
+        dma((3,)),
+        dma((3,)),
+        dma((slots + 1,)),
+        dma((slots + 1,)),
+        dma((1,)),
+        dma((1,)),
+        dma((3,)),
+        dma((3,)),
+        dma((3,)),
+        dma((3,)),
+        dma((2,)),
+        dma((2,)),
     ]
     shape = jax.ShapeDtypeStruct((outs, slab), F32)
     return tuple(

time: 89.3 us -> 84.1 us (0.942)
  Pallas kernels: 83.7 us -> 78.5 us
    pallas_call x1, Pallas kernels: 83.7 us -> 78.5 us  [body(): pl.pallas_call(functools.partial(solve_kernel, rows, cols, halo), out_sha...]
where the time goes in v4:
time: 84.1 us; the launch traced here: 83.9 us
  Pallas kernels  78.5 us (93%)
  local copies, waits for them, and re-layouts  3.82 us (5%)
  other arithmetic  0.86 us (1%)
    pallas_call x1, Pallas kernels, body(): pl.pallas_call(functools.partial(solve_kernel, rows, cols, halo), out_sha...  78.5 us
    unnamed x9, local copies, waits for them, and re-layouts  2.89 us

profile of v4, /device:TPU:1, one launch (start us, length us, event | category | flops | bytes accessed | tf_op | source)
XLA Modules:
  0.0 83.9 jit_solution(18052818033283288290)
XLA Ops:
  0.6 0.0 copy-start.1
  0.6 0.0 copy-start.2
  0.7 0.0 copy-start
  0.7 0.7 and_convert_fusion
  1.4 1.5 %copy.9 = f32[3,4096]{0,1:T(8,128)S(1)} copy(f32[3,4096]{1,0:T(4,128)} %param.6) | data formatting | bytes 98304 | tf_op args[0]
  2.9 0.7 gather_fusion
  3.6 0.1 copy.10
  3.8 0.1 pad.2.clone
  3.8 0.0 copy-done.1
  3.8 0.0 copy-done.2
  3.8 0.1 pad_maximum_fusion
  4.0 0.0 copy-done
  4.0 78.5 %shard_map.59 = (f32[16,4096]{1,0:T(8,128)S(1)}, f32[16,4096]{1,0:T(8,128)S(1)}) custom-call(f32[16,24,256]{2,1,0:T(8,128)S(1)} %bitcast.9, f32[4,256]{1,0:T(4,128)S(1)} %concatenate.7.picked, f32[8,256]{1,0:T(8,128)S(1)} %broadcast_in_dim.41.close, f32[256,256]{1,0:T(8,128)S(1)} %copy-done), custom_call_target="tpu_custom_call" | custom-call | tf_op jit(solution)/shard_map/pallas_call | solution.py:623
  82.5 0.7 copy.16
  83.2 0.7 copy.17
  (6 shorter events, 0.1 us)
Async XLA Ops:
  0.6 3.2 %copy-start.1 = (f32[3,4096]{1,0:T(4,128)S(1)}, f32[3,4096]{1,0:T(4,128)}, u32[]{:S(2)}) copy-start(f32[3,4096]{1,0:T(4,128)} %param.6) | copy-start | bytes 147460
  0.6 3.2 %copy-start.2 = (f32[16,4096]{1,0:T(8,128)S(1)}, f32[16,4096]{1,0:T(8,128)}, u32[]{:S(2)}) copy-start(f32[16,4096]{1,0:T(8,128)} %param.7) | copy-start | bytes 786436
  0.7 3.3 %copy-start = (f32[256,256]{1,0:T(8,128)S(1)}, f32[256,256]{1,0:T(8,128)}, u32[]{:S(2)}) copy-start(f32[256,256]{1,0:T(8,128)} %core.1) | copy-start | bytes 786436

commit v5 on v4

--- a/solution.py
+++ b/solution.py
@@ -406,6 +406,11 @@
 
     image_message = message(product(q0, own_high[...], own_low[...]), [dots(z0_own, q0)])
 
+    far_cut = (slots - near) // 3
+
+    def far_mark(i):
+        mark_slot(lax.rem(c + near + i, slots))
+
     def send_first():
         edge_peers(
             lambda index, row, col, slot: q_copy(
@@ -413,17 +418,18 @@
             ).start()
         )
         loop(cols, lambda i: q_copy(slots, r, col_peer(i), own, slots).start(), 1)
-        loop(slots - near, lambda i: mark_slot(lax.rem(c + near + i, slots)))
+        loop(far_cut, far_mark)
 
     def first_slab(i):
         z_first[i] = first_z(halo + i)
 
     def take_first():
+        loop(cols, first_slab)
         edge_peers(lambda index, row, col, slot: q_copy(index, row, col, slot).wait_recv())
         q_done().wait_recv()
 
     sums = total(
-        1, image_message, send_first, lambda: loop(cols, first_slab), take_first
+        1, image_message, send_first, lambda: loop(slots - near, far_mark, far_cut), take_first
     )
 
     curve0 = sums[:, width : width + 1]

time: 84.1 us -> 83.9 us (level)
  no operation moved by 1% of the time
where the time goes in v5:
time: 83.9 us; the launch traced here: 83.8 us
  Pallas kernels  78.4 us (93%)
  local copies, waits for them, and re-layouts  3.82 us (5%)
  other arithmetic  0.86 us (1%)
    pallas_call x1, Pallas kernels, body(): pl.pallas_call(functools.partial(solve_kernel, rows, cols, halo), out_sha...  78.4 us
    unnamed x9, local copies, waits for them, and re-layouts  2.89 us

profile of v5, /device:TPU:1, one launch (start us, length us, event | category | flops | bytes accessed | tf_op | source)
XLA Modules:
  0.0 83.8 jit_solution(8302098161872434737)
XLA Ops:
  0.6 0.0 copy-start.1
  0.6 0.0 copy-start.2
  0.7 0.0 copy-start
  0.7 0.7 and_convert_fusion
  1.4 1.5 %copy.9 = f32[3,4096]{0,1:T(8,128)S(1)} copy(f32[3,4096]{1,0:T(4,128)} %param.6) | data formatting | bytes 98304 | tf_op args[0]
  2.9 0.7 gather_fusion
  3.6 0.1 copy.10
  3.8 0.1 pad.2.clone
  3.8 0.0 copy-done.1
  3.8 0.0 copy-done.2
  3.8 0.1 pad_maximum_fusion
  4.0 0.0 copy-done
  4.0 78.4 %shard_map.59 = (f32[16,4096]{1,0:T(8,128)S(1)}, f32[16,4096]{1,0:T(8,128)S(1)}) custom-call(f32[16,24,256]{2,1,0:T(8,128)S(1)} %bitcast.9, f32[4,256]{1,0:T(4,128)S(1)} %concatenate.7.picked, f32[8,256]{1,0:T(8,128)S(1)} %broadcast_in_dim.41.close, f32[256,256]{1,0:T(8,128)S(1)} %copy-done), custom_call_target="tpu_custom_call" | custom-call | tf_op jit(solution)/shard_map/pallas_call | solution.py:629
  82.4 0.7 copy.16
  83.1 0.7 copy.17
  (6 shorter events, 0.1 us)
Async XLA Ops:
  0.6 3.2 %copy-start.1 = (f32[3,4096]{1,0:T(4,128)S(1)}, f32[3,4096]{1,0:T(4,128)}, u32[]{:S(2)}) copy-start(f32[3,4096]{1,0:T(4,128)} %param.6) | copy-start | bytes 147460
  0.6 3.2 %copy-start.2 = (f32[16,4096]{1,0:T(8,128)S(1)}, f32[16,4096]{1,0:T(8,128)}, u32[]{:S(2)}) copy-start(f32[16,4096]{1,0:T(8,128)} %param.7) | copy-start | bytes 786436
  0.7 3.3 %copy-start = (f32[256,256]{1,0:T(8,128)S(1)}, f32[256,256]{1,0:T(8,128)}, u32[]{:S(2)}) copy-start(f32[256,256]{1,0:T(8,128)} %core.1) | copy-start | bytes 786436
